TPU v7x, 128 devices: a whole 4x4x4 slice. The times are simulated.
128 devices in a mesh: comp: 2 (over z_hi), mr: 64 (over z_lo, y, x, core).
Axes of the slice: x: 4, y: 4, z: 4 (z_hi: 2, z_lo: 2; z = z_hi * 2 + z_lo), core: 2. Of those that a mesh axis runs over, the one named last changes fastest.
Arguments:
- spectrum: float32 [2, 1024, 2, 64, 512], P('comp', 'mr'), may hold values from -6 to 6
- radial_basis: bfloat16 [1024, 1024, 512], P('mr'), may hold values from -0.25 to 0.25
- cutoff: int32 [1024], P('mr'), may hold values from 128 to 512, as said below
- couplings: float32 [2, 2], replicated, may hold values from 0.5 to 1.5
- trap_potential: float32 [1024], replicated, may hold values from 0 to 2
- weights: float32 [1024], replicated, may hold values from 0.25 to 0.75
Outputs:
- evolved: float32 [2, 1024, 2, 64, 512], P('comp', 'mr')
Inputs may be any that keep to these rules, and one draw needn't show every extreme that they name: cutoff[m] is the number of Laguerre degrees kept for angular mode m; degrees from cutoff[m] on are dropped.
All inputs are finite; a program needn't handle non-finite values.
Results may differ from a plain program's by a relative error of at most 0.0089.
Values may be sent and summed in bfloat16 or wider, within the bound.
A program may use at most 128 MiB of HBM per device.

v0:
```python
import functools
import math

import jax
import jax.numpy as jnp
import ml_dtypes
import numpy as np
from jax import lax
from jax.experimental import pallas as pl
from jax.experimental.pallas import tpu as pltpu
from jax.sharding import PartitionSpec as P

TIMESTEP = 0.5
ROTATION = 0.7
MESH = pl.DeviceIdType.MESH
CHUNKS = 4
GROUPS = 4
QUARTERS = 4
F32 = jnp.float32
BF16 = jnp.bfloat16


def quarter_tables(mode_total):
    quarter = mode_total // QUARTERS
    angle = QUARTERS * np.arange(quarter)[None, :, None] + np.arange(QUARTERS)[:, None, None]
    product = angle * np.arange(quarter)[None, None, :] % mode_total
    turn = product * (2.0 * math.pi / mode_total)
    both = np.stack([np.cos(turn), np.sin(turn)], 1) / math.sqrt(mode_total)
    both = both.astype(np.float32).astype(ml_dtypes.bfloat16)
    return np.stack([both, both.swapaxes(-1, -2)])


def sine_cosine(angle):
    turns = jnp.round(angle * (2.0 / math.pi))
    rest = angle - turns * 1.5703125
    rest = rest - turns * 4.837512969970703125e-4
    rest = rest - turns * 7.54978995489188e-8
    rest = jnp.clip(rest, -0.8, 0.8)
    square = rest * rest
    sine = ((-1.9515295891e-4 * square + 8.3321608736e-3) * square - 1.6666654611e-1) * square
    sine = sine * rest + rest
    cosine = (2.443315711809948e-5 * square - 1.388731625493765e-3) * square
    cosine = (cosine + 4.166664568298827e-2) * square * square - 0.5 * square + 1.0
    corner = (turns - 4.0 * jnp.floor(turns * 0.25)).astype(jnp.int32)
    swap = (corner & 1) == 1
    sine, cosine = jnp.where(swap, cosine, sine), jnp.where(swap, sine, cosine)
    sine = jnp.where(corner >= 2, -sine, sine)
    cosine = jnp.where((corner == 1) | (corner == 2), -cosine, cosine)
    return sine, cosine


def sine_cosine_of_turns(turns):
    rest = turns - jnp.round(turns)
    square = rest * rest
    twice = 0.1553153206018442 * square - 1.1965825712357152
    twice = (twice * square + 5.100155046428268) * square - 10.335420167015725
    twice = (twice * square + 6.283185280261414) * rest
    cosine = 0.2196896110917421 * square - 1.3318765680776314
    cosine = (cosine * square + 4.058411352862034) * square - 4.93479283061961
    cosine = cosine * square + 0.9999999532476082
    return twice * cosine, 1.0 - 0.5 * (twice * twice)


def kernel(
    cutoff_hbm, couplings_hbm, trap_hbm, weights_hbm, spectrum_hbm, basis_hbm, tables_hbm, total,
    basis, coeffs, tables, forward, inverse, sent, landed, sent_back, landed_back,
    stage, turned, field, kicked, modes, wave_cos, wave_sin,
    cutoff, couplings, trap, weights, load_sem, scalar_sem, spectrum_sem, first_sem, basis_sem, send_sem, recv_sem, send_back_sem, recv_back_sem,
):
    comps, group = lax.axis_size("comp"), lax.axis_size("mr")
    comp, place = lax.axis_index("comp"), lax.axis_index("mr")
    devices = comps * group
    me = comp * group + place
    local = coeffs.shape[0]
    planes = coeffs.shape[1] // 2
    degrees = coeffs.shape[2]
    rows = basis.shape[2]
    half = rows // 2
    quarter = forward.shape[1] // 2
    quarter_places = group // QUARTERS
    mode_total = local * group
    pair = 2 * local

    digits = lax.div(me, 32), lax.rem(lax.div(me, 8), 4), lax.rem(lax.div(me, 2), 4), lax.rem(me, 2)
    layers = [lax.rem(digits[0] + near, 4) for near in range(4)]
    cores = [digits[3], 1 - digits[3]]

    def visit(outer, skip_self, act):
        y, x = digits[1] + lax.rem(outer, 4), digits[2] + lax.div(outer, 4)
        for near in range(4):
            column = lax.rem(y + near, 4) * 8 + lax.rem(x + near, 4) * 2
            side = lax.div(layers[near], 2)
            spot = layers[near] * 32 - side * group + column
            for core in range(2):
                if not (skip_self and near == 0 and core == 0):
                    act(side, spot + cores[core])

    def visit_others(act):
        visit(0, True, act)

        def one(outer, carry):
            visit(outer, False, act)
            return carry

        lax.fori_loop(1, devices // 8, one, 0)

    portion = local // GROUPS

    def spectrum_copy(g):
        some = pl.ds(g * portion, portion)
        return pltpu.make_async_copy(spectrum_hbm.at[some], total.at[some], spectrum_sem.at[g])

    def first_copy(g):
        some = pl.ds(g * portion, portion)
        return pltpu.make_async_copy(
            basis_hbm.at[some, pl.ds(0, rows), :], basis.at[0, some], first_sem.at[g]
        )

    for g in range(GROUPS):
        spectrum_copy(g).start()
        first_copy(g).start()

    scalar_copies = [
        pltpu.make_async_copy(source, target, scalar_sem.at[i])
        for i, (source, target) in enumerate(
            (
                (cutoff_hbm, cutoff),
                (couplings_hbm, couplings),
                (trap_hbm, trap),
                (weights_hbm, weights),
            )
        )
    ]
    for copy in scalar_copies:
        copy.start()

    def basis_copy(k):
        return pltpu.make_async_copy(
            basis_hbm.at[:, pl.ds(k * rows, rows), :], basis.at[k], basis_sem.at[k]
        )

    barrier = pltpu.get_barrier_semaphore()

    def greet(side, spot):
        pl.semaphore_signal(
            barrier, inc=1, device_id={"comp": side, "mr": spot}, device_id_type=MESH
        )

    visit_others(greet)
    tables_copy = pltpu.make_async_copy(tables_hbm, tables, load_sem)
    for k in range(1, CHUNKS):
        basis_copy(k).start()
    tables_copy.start()

    lane = lax.broadcasted_iota(jnp.int32, (1, 2 * planes), 1)
    first = lane < planes
    degree_ids = lax.broadcasted_iota(jnp.int32, (1, degrees), 1)

    mode_ids = place * local + lax.broadcasted_iota(jnp.int32, (local, 1), 0)
    signed = jnp.where(mode_ids < mode_total // 2, mode_ids, mode_ids - mode_total).astype(F32)
    energy = 2.0 * degree_ids.astype(F32) + (jnp.abs(signed) + 1.0 - ROTATION * signed)
    wave_sin[...], wave_cos[...] = sine_cosine(TIMESTEP * energy)

    def spin(m, carry):
        kept = jnp.where(degree_ids < cutoff[m], 1.0, 0.0)
        cosine, sine = wave_cos[pl.ds(m, 1), :] * kept, wave_sin[pl.ds(m, 1), :] * kept
        real, imag = total[m, 0:planes, :], total[m, planes:, :]
        coeffs[m, 0:planes, :] = (real * cosine + imag * sine).astype(BF16)
        coeffs[m, planes:, :] = (imag * cosine - real * sine).astype(BF16)
        return carry


    def swap_halves(low, high):
        return (
            jnp.where(first, low, pltpu.roll(high, planes, 1)),
            jnp.where(first, pltpu.roll(low, planes, 1), high),
        )

    def scatter(source, target, send, recv, k):
        def go(side, spot):
            pltpu.make_async_remote_copy(
                src_ref=source.at[k, side * group + spot],
                dst_ref=target.at[k, me],
                send_sem=send.at[k],
                recv_sem=recv.at[k],
                device_id={"comp": side, "mr": spot},
                device_id_type=MESH,
            ).start()

        visit_others(go)
        target[k, me] = source[k, me]

    def drain(buffer, sem, k):
        others = buffer.at[k, pl.ds(0, devices - 1)]
        pltpu.make_async_copy(others, others, sem.at[k]).wait()

    def one_mode(k, m):
        values = lax.dot_general(
            basis[k, m], coeffs[m], (((1,), (1,)), ((), ())), preferred_element_type=F32
        )
        real, imag = swap_halves(values[:half], values[half:])
        stage[pl.ds(m, devices, stride=pair), :] = real
        stage[pl.ds(local + m, devices, stride=pair), :] = imag

    def pack_all(k):
        def pack(b, carry):
            block = stage[pl.ds(pl.multiple_of(b * 8 * pair, 8 * pair), 8 * pair), :]
            sent[k, pl.ds(b * 8, 8)] = block.astype(BF16).reshape(8, pair, 2 * planes)
            return carry

        lax.fori_loop(0, devices // 8, pack, 0, unroll=2)

    def begin(g, carry):
        spectrum_copy(g).wait()
        for i in range(portion):
            spin(g * portion + i, 0)
        first_copy(g).wait()
        for i in range(portion):
            one_mode(0, g * portion + i)
        return carry

    for copy in scalar_copies:
        copy.wait()
    lax.fori_loop(0, GROUPS, begin, 0)
    pack_all(0)
    pl.semaphore_wait(barrier, devices - 1)
    scatter(sent, landed, send_sem, recv_sem, 0)

    def outward(k, carry):
        basis_copy(k).wait()

        def one(m, carry):
            one_mode(k, m)
            return carry

        lax.fori_loop(0, local, one, 0, unroll=4)
        pack_all(k)
        scatter(sent, landed, send_sem, recv_sem, k)
        return carry

    lax.fori_loop(1, CHUNKS, outward, 0)

    tables_copy.wait()
    low, high = pl.ds(0, quarter), pl.ds(quarter, quarter)
    for table, index, sign in ((forward, 0, 1), (inverse, 1, -1)):
        for s in range(QUARTERS):
            cosine, sine = tables[index, s, 0], tables[index, s, 1]
            table[s, low, low] = cosine
            table[s, high, high] = cosine
            table[s, high, low] = sine * sign
            table[s, low, high] = sine * -sign

    def physical(k):
        def radix_in(b, carry):
            for c in range(comps):
                x = []
                for h in range(QUARTERS):
                    tile = landed[k, c * group + h * quarter_places + b].astype(F32)
                    x.append((tile[:local], tile[local:]))
                (ar, ai), (br, bi) = [
                    (x[h][0] + x[h + 2][0], x[h][1] + x[h + 2][1]) for h in range(2)
                ]
                (er, ei), (fr, fi) = [
                    (x[h][0] - x[h + 2][0], x[h][1] - x[h + 2][1]) for h in range(2)
                ]
                mixed = (
                    (ar + br, ai + bi), (er - fi, ei + fr), (ar - br, ai - bi), (er + fi, ei - fr)
                )
                columns = pl.ds(c * 2 * planes, 2 * planes)
                start = pl.multiple_of(b * local, local)
                for s in range(QUARTERS):
                    turned[s, pl.ds(start, local), columns] = mixed[s][0].astype(BF16)
                    turned[s, pl.ds(quarter + start, local), columns] = mixed[s][1].astype(BF16)
            return carry

        lax.fori_loop(0, quarter_places, radix_in, 0, unroll=2)
        radius = k * rows + me
        scale = TIMESTEP / (2.0 * math.pi)
        own = [couplings[c, 0] * scale for c in range(comps)]
        other = [couplings[c, 1] * scale for c in range(comps)]
        potential = jnp.where(first, trap[radius], trap[radius + half]) * scale
        measure = jnp.where(first, weights[radius], weights[radius + half])

        def transform(s, carry):
            field[...] = jnp.dot(forward[s], turned[s], preferred_element_type=F32)

            def kick(b, carry):
                start = pl.multiple_of(b * 32, 32)
                psi = []
                for c in range(comps):
                    columns = pl.ds(c * 2 * planes, 2 * planes)
                    psi.append(
                        (field[pl.ds(start, 32), columns], field[pl.ds(quarter + start, 32), columns])
                    )
                density = [real * real + imag * imag for real, imag in psi]
                for c in range(comps):
                    columns = pl.ds(c * 2 * planes, 2 * planes)
                    turns = own[c] * density[c] + other[c] * density[1 - c] + potential
                    sine, cosine = sine_cosine_of_turns(turns)
                    real, imag = psi[c]
                    kicked[pl.ds(start, 32), columns] = (real * cosine + imag * sine).astype(BF16)
                    kicked[pl.ds(quarter + start, 32), columns] = (
                        imag * cosine - real * sine
                    ).astype(BF16)
                return carry

            lax.fori_loop(0, quarter // 32, kick, 0, unroll=2)
            modes[s] = jnp.dot(inverse[s], kicked[...], preferred_element_type=F32)
            return carry

        lax.fori_loop(0, QUARTERS, transform, 0)

        def radix_out(b, carry):
            start = pl.multiple_of(b * local, local)
            for c in range(comps):
                columns = pl.ds(c * 2 * planes, 2 * planes)
                x = [
                    (
                        modes[s, pl.ds(start, local), columns],
                        modes[s, pl.ds(quarter + start, local), columns],
                    )
                    for s in range(QUARTERS)
                ]
                (ar, ai), (br, bi) = [
                    (x[h][0] + x[h + 2][0], x[h][1] + x[h + 2][1]) for h in range(2)
                ]
                (er, ei), (fr, fi) = [
                    (x[h][0] - x[h + 2][0], x[h][1] - x[h + 2][1]) for h in range(2)
                ]
                mixed = (
                    (ar + br, ai + bi), (er + fi, ei - fr), (ar - br, ai - bi), (er - fi, ei + fr)
                )
                for h in range(QUARTERS):
                    device = c * group + h * quarter_places + b
                    sent_back[k, device, 0:local, :] = (mixed[h][0] * measure).astype(BF16)
                    sent_back[k, device, local:, :] = (mixed[h][1] * measure).astype(BF16)
            return carry

        lax.fori_loop(0, quarter_places, radix_out, 0, unroll=2)

    def analyze(k, starts, last):
        drain(landed_back, recv_back_sem, k)

        def unpack(b, carry):
            block = landed_back[k, pl.ds(b * 8, 8)].astype(F32)
            stage[pl.ds(pl.multiple_of(b * 8 * pair, 8 * pair), 8 * pair), :] = block.reshape(
                8 * pair, 2 * planes
            )
            return carry

        lax.fori_loop(0, devices // 8, unpack, 0, unroll=2)

        def one(m, carry):
            parts = []
            for p in range(2):
                block = stage[pl.ds(p * local + m, devices, stride=pair), :].T.astype(BF16)
                parts.append(jnp.concatenate([block[:planes], block[planes:]], 1))
            values = jnp.dot(jnp.concatenate(parts, 0), basis[k, m], preferred_element_type=F32)
            if not starts:
                values = total[m] + values
            if last:
                values = values * jnp.where(degree_ids < cutoff[m], 1.0, 0.0)
            total[m] = values
            return carry

        lax.fori_loop(0, local, one, 0, unroll=4)

    def back(k, carry):
        drain(landed, recv_sem, k)
        physical(k)
        scatter(sent_back, landed_back, send_back_sem, recv_back_sem, k)
        return carry

    def gather(k, carry):
        analyze(k, False, False)
        return carry

    lax.fori_loop(0, CHUNKS, back, 0)
    analyze(0, True, False)
    lax.fori_loop(1, CHUNKS - 1, gather, 0)
    analyze(CHUNKS - 1, False, True)

    def finish(k, carry):
        drain(sent, send_sem, k)
        drain(sent_back, send_back_sem, k)
        return carry

    lax.fori_loop(0, CHUNKS, finish, 0)


def on_device(spectrum, radial_basis, cutoff, couplings, trap_potential, weights):
    local_modes, _, planes, degrees = spectrum.shape[1:]
    radius_count = radial_basis.shape[1]
    devices = lax.axis_size("comp") * lax.axis_size("mr")
    mode_total = local_modes * lax.axis_size("mr")
    rows = radius_count // CHUNKS
    width = 2 * planes
    quarter = mode_total // QUARTERS
    pair = 2 * local_modes
    comps = lax.axis_size("comp")
    blocks = pltpu.VMEM((CHUNKS, devices, pair, width), BF16)
    outside = pl.BlockSpec(memory_space=pltpu.HBM)
    evolved = pl.pallas_call(
        kernel,
        out_shape=jax.ShapeDtypeStruct((local_modes, width, degrees), F32),
        in_specs=[outside] * 7,
        out_specs=pl.BlockSpec(memory_space=pltpu.VMEM),
        scratch_shapes=[
            pltpu.VMEM((CHUNKS, local_modes, rows, degrees), BF16),
            pltpu.VMEM((local_modes, width, degrees), BF16),
            pltpu.VMEM((2, QUARTERS, 2, quarter, quarter), BF16),
            pltpu.VMEM((QUARTERS, 2 * quarter, 2 * quarter), BF16),
            pltpu.VMEM((QUARTERS, 2 * quarter, 2 * quarter), BF16),
            blocks,
            blocks,
            blocks,
            blocks,
            pltpu.VMEM((devices * pair, width), F32),
            pltpu.VMEM((QUARTERS, 2 * quarter, comps * width), BF16),
            pltpu.VMEM((2 * quarter, comps * width), F32),
            pltpu.VMEM((2 * quarter, comps * width), BF16),
            pltpu.VMEM((QUARTERS, 2 * quarter, comps * width), F32),
            pltpu.VMEM((local_modes, degrees), F32),
            pltpu.VMEM((local_modes, degrees), F32),
            pltpu.SMEM((local_modes,), jnp.int32),
            pltpu.SMEM((comps, comps), F32),
            pltpu.SMEM((radius_count,), F32),
            pltpu.SMEM((radius_count,), F32),
            pltpu.SemaphoreType.DMA,
            pltpu.SemaphoreType.DMA((4,)),
            pltpu.SemaphoreType.DMA((GROUPS,)),
            pltpu.SemaphoreType.DMA((GROUPS,)),
            pltpu.SemaphoreType.DMA((CHUNKS,)),
            pltpu.SemaphoreType.DMA((CHUNKS,)),
            pltpu.SemaphoreType.DMA((CHUNKS,)),
            pltpu.SemaphoreType.DMA((CHUNKS,)),
            pltpu.SemaphoreType.DMA((CHUNKS,)),
        ],
        compiler_params=pltpu.CompilerParams(collective_id=0, has_side_effects=True, vmem_limit_bytes=47 << 20),
    )(
        *[
            pltpu.with_memory_space_constraint(x, pltpu.HBM)
            for x in (
                cutoff,
                couplings,
                trap_potential,
                weights,
                spectrum.reshape(local_modes, width, degrees),
                radial_basis,
                jnp.asarray(quarter_tables(mode_total)),
            )
        ]
    )
    return evolved.reshape(1, local_modes, 2, planes, degrees)


def solution(mesh):
    in_specs = (P("comp", "mr", None, None, None), P("mr", None, None), P("mr"), P(), P(), P())
    out_specs = P("comp", "mr", None, None, None)
    return jax.shard_map(
        on_device, mesh=mesh, in_specs=in_specs, out_specs=out_specs, check_vma=False
    )
```

profile of v0, /device:TPU:1, one launch (start us, length us, event | category | flops | bytes accessed | tf_op | source)
XLA Modules:
  0.0 109.6 jit_solution(8750583271895118900)
XLA Ops:
  0.0 107.6 %shard_map.73 = f32[16,128,512]{2,1,0:T(8,128)S(1)} custom-call(s32[16]{0:T(128)} %cutoff_hbm.1, f32[2,2]{1,0:T(2,128)} %couplings_hbm.1, f32[1024]{0:T(1024)} %trap_hbm.1, f32[1024]{0:T(1024)} %weights_hbm.1, f32[16,128,512]{2,1,0:T(8,128)} %bitcast.3, bf16[16,1024,512]{2,1,0:T(8,128)(2,1)} %basis_hbm.1, bf16[2,4,2,256,256]{4,3,2,1,0:T(8,128)(2,1)} %constant.2.clone.tables_hbm), custom_call_target="tpu_custom_call" | custom-call | tf_op jit(solution)/shard_map/pallas_call | solution.py:403
  107.6 2.0 %copy.9 = f32[1,16,2,64,512]{4,3,2,1,0:T(8,128)} copy(f32[1,16,2,64,512]{4,3,2,1,0:T(8,128)S(1)} %bitcast.2) | data formatting | bytes 8388608
where the time goes:
time: 110 us
  Pallas kernels  108 us (98%)
  local copies, waits for them, and re-layouts  2.02 us (2%)
    pallas_call x1, Pallas kernels, on_device(): pl.pallas_call(kernel, out_shape=jax.ShapeDtypeStruct((local_modes, width...  108 us

commit v1 on v0

--- a/solution.py
+++ b/solution.py
@@ -233,7 +233,7 @@
             one_mode(k, m)
             return carry
 
-        lax.fori_loop(0, local, one, 0, unroll=4)
+        lax.fori_loop(0, local, one, 0, unroll=8)
         pack_all(k)
         scatter(sent, landed, send_sem, recv_sem, k)
         return carry
@@ -363,7 +363,7 @@
             total[m] = values
             return carry
 
-        lax.fori_loop(0, local, one, 0, unroll=4)
+        lax.fori_loop(0, local, one, 0, unroll=8)
 
     def back(k, carry):
         drain(landed, recv_sem, k)

time: 110 us -> 110 us (level)
  no operation moved by 1% of the time
where the time goes in v1:
time: 110 us; the launch traced here: 109 us
  Pallas kernels  107 us (97%)
  local copies, waits for them, and re-layouts  2.02 us (2%)
    pallas_call x1, Pallas kernels, on_device(): pl.pallas_call(kernel, out_shape=jax.ShapeDtypeStruct((local_modes, width...  107 us

profile of v1, /device:TPU:1, one launch (start us, length us, event | category | flops | bytes accessed | tf_op | source)
XLA Modules:
  0.0 109.4 jit_solution(14544180021912866857)
XLA Ops:
  0.0 107.4 %shard_map.73 = f32[16,128,512]{2,1,0:T(8,128)S(1)} custom-call(s32[16]{0:T(128)} %cutoff_hbm.1, f32[2,2]{1,0:T(2,128)} %couplings_hbm.1, f32[1024]{0:T(1024)} %trap_hbm.1, f32[1024]{0:T(1024)} %weights_hbm.1, f32[16,128,512]{2,1,0:T(8,128)} %bitcast.3, bf16[16,1024,512]{2,1,0:T(8,128)(2,1)} %basis_hbm.1, bf16[2,4,2,256,256]{4,3,2,1,0:T(8,128)(2,1)} %constant.2.clone.tables_hbm), custom_call_target="tpu_custom_call" | custom-call | tf_op jit(solution)/shard_map/pallas_call | solution.py:403
  107.4 2.0 %copy.9 = f32[1,16,2,64,512]{4,3,2,1,0:T(8,128)} copy(f32[1,16,2,64,512]{4,3,2,1,0:T(8,128)S(1)} %bitcast.2) | data formatting | bytes 8388608
